TPU v7x, 32 devices: a whole 2x2x4 slice. The times are simulated.
32 devices in a mesh: bus: 8 (over y, x, core), period: 4 (over z).
Axes of the slice: x: 2, y: 2, z: 4, core: 2. Of those that a mesh axis runs over, the one named last changes fastest.
Arguments:
- deviation: bfloat16 [128, 256, 128], P('bus', 'period'), may hold values from -6 to 6
- loading: bfloat16 [128, 256, 128], P('bus', 'period'), may hold values from 0.5 to 2
- jacobian: bfloat16 [128, 128, 128], P('bus'), may hold values from -0.5 to 0.5
- tie_source: int32 [128, 16], P('bus'), may hold values from 0 to 127
- tie_target: int32 [128, 16], P('bus'), may hold values from 0 to 127
- tie_admittance: float32 [128, 16], P('bus'), may hold values from 0.5 to 2
- condense: bfloat16 [128, 128, 512], P('bus'), may hold values from -0.046875 to 0.046875
- section_gain: bfloat16 [4, 64, 512, 512], P('period', 'bus'), may hold values from -0.0625 to 0.0625
- retention: float32 [4, 64, 512], P('period', 'bus'), may hold values from 0 to 1
Outputs:
- mismatch: bfloat16 [128, 256, 128], P('bus', 'period')
- section_states: float32 [4, 64, 512], P('period', 'bus')
All inputs are finite; a program needn't handle non-finite values.
Results may differ from a plain program's by a relative error of at most 0.013.
Values may be sent and summed in bfloat16 or wider, within the bound.
No kernel may reach another device: no remote copies, remote signals or barrier semaphores. Data moves between devices by JAX's collectives and lax.ppermute only.
A program may use at most 64 MiB of HBM per device.

v0:
```python
import jax
import jax.numpy as jnp
from jax import lax
from jax.sharding import PartitionSpec as P


def from_behind(value, axis, steps):
    count = lax.axis_size(axis)
    leading, last = (max(0, -steps), min(count, count - steps))
    return lax.ppermute(value, axis, [(source, source + steps) for source in range(leading, last)])


def entering_2(value, axis, combine, identity):
    size, place = (lax.axis_size(axis), lax.axis_index(axis))
    everything = jax.tree.map(lambda part: lax.all_gather(part, axis), value)
    start = jax.tree.map(
        lambda part, zero: jnp.broadcast_to(jnp.asarray(zero, part.dtype), part.shape),
        value,
        identity,
    )

    def step(k, before):
        reached = k < place
        new = combine(before, jax.tree.map(lambda part: part[k], everything))
        return jax.tree.map(lambda a, b: jnp.where(reached, a, b), new, before)

    return lax.fori_loop(0, size, step, start)


def broadcast(block, axis, owner):
    block = jnp.where(lax.axis_index(axis) == owner, block, jnp.zeros_like(block))
    return lax.psum(block, axis)


def combine(earlier, later):
    return (earlier[0] * later[0], later[0] * earlier[1] + later[1])


def place(flows, hot):
    upper = flows.astype(jnp.bfloat16)
    lower = (flows - upper.astype(jnp.float32)).astype(jnp.bfloat16)
    both = jnp.concatenate([upper, lower], axis=2)
    hot_twice = jnp.concatenate([hot, hot], axis=1)
    return jnp.einsum("bte,beq->btq", both, hot_twice, preferred_element_type=jnp.float32)


def shards(
    deviation,
    loading,
    jacobian,
    tie_source,
    tie_target,
    tie_admittance,
    condense,
    section_gain,
    retention,
):
    block_width = deviation.shape[2]
    scaled = (deviation.astype(jnp.float32) * loading.astype(jnp.float32)).astype(jnp.bfloat16)
    columns = jnp.arange(block_width, dtype=jnp.int32)
    source_hot = (tie_source[:, :, None] == columns[None, None, :]).astype(jnp.bfloat16)
    target_hot = (tie_target[:, :, None] == columns[None, None, :]).astype(jnp.bfloat16)
    next_first = from_behind(scaled[0], "bus", -1)
    next_block = jnp.concatenate([scaled[1:], next_first[None]], axis=0)
    at_target = jnp.einsum(
        "btq,beq->bte", next_block, target_hot, preferred_element_type=jnp.float32
    )
    network = jnp.einsum("btp,bpq->btq", scaled, jacobian, preferred_element_type=jnp.float32)
    at_source = jnp.einsum("btq,beq->bte", scaled, source_hot, preferred_element_type=jnp.float32)
    edge_flow = tie_admittance[:, None, :] * (at_target - at_source)
    own_terms = place(edge_flow, source_hot)
    handed = -place(edge_flow, target_hot)
    incoming = from_behind(handed[-1], "bus", 1)
    received = jnp.concatenate([incoming[None], handed[:-1]], axis=0)
    mismatch = (network + own_terms + received).astype(jnp.bfloat16)
    span_rows = section_gain.shape[1]
    partial_value = jnp.einsum(
        "btq,bqm->tm", mismatch, condense, preferred_element_type=jnp.float32
    )
    totals = lax.psum(partial_value, "bus")
    section_sum = lax.dynamic_slice_in_dim(totals, lax.axis_index("bus") * span_rows, span_rows, 0)
    section_in = section_sum.astype(jnp.bfloat16)
    pushed = jnp.einsum(
        "tm,tmn->tn", section_in, section_gain[0], preferred_element_type=jnp.float32
    )
    states_width = pushed.shape[1]
    ones_row = jnp.ones((states_width,), jnp.float32)
    zeros_row = jnp.zeros((states_width,), jnp.float32)

    def advance(carried, inputs):
        section_now, product = carried
        retain, pushed_now = inputs
        section_now = retain * section_now + pushed_now
        product = product * retain
        return ((section_now, product), (section_now, product))

    (last_state, span_rate), (local_states, running) = lax.scan(
        advance, (zeros_row, ones_row), (retention[0], pushed)
    )
    own_map = (span_rate, last_state)
    identity = (ones_row, zeros_row)
    before = entering_2(own_map, "bus", combine, identity)
    through = combine(before, own_map)
    group_map = (
        broadcast(through[0], "bus", lax.axis_size("bus") - 1),
        broadcast(through[1], "bus", lax.axis_size("bus") - 1),
    )
    across = entering_2(group_map, "period", combine, identity)
    entering = combine(across, before)[1]
    states = local_states + running * entering[None, :]
    return (mismatch, states[None])


def solution(mesh):
    placed = (
        P("bus", "period", None),
        P("bus", "period", None),
        P("bus", None, None),
        P("bus", None),
        P("bus", None),
        P("bus", None),
        P("bus", None, None),
        P("period", "bus", None, None),
        P("period", "bus", None),
    )
    return jax.shard_map(
        shards,
        mesh=mesh,
        in_specs=placed,
        out_specs=(P("bus", "period", None), P("period", "bus", None)),
        check_vma=False,
    )
```

profile of v0, /device:TPU:0, one launch (start us, length us, event | category | flops | bytes accessed | tf_op | source)
XLA Modules:
  0.0 106.2 jit_solution(14670595446566683150)
XLA Ops:
  0.6 0.0 copy-start
  0.6 0.0 copy-start.2
  0.7 1.3 %multiply_convert_fusion = bf16[16,64,128]{2,1,0:T(8,128)(2,1)S(1)} fusion(bf16[16,64,128]{2,1,0:T(8,128)(2,1)} %param.16, bf16[16,64,128]{2,1,0:T(8,128)(2,1)} %param.15), kind=kLoop, calls=%fused_computation.21 | loop fusion | flops 524288 | bytes 786432 | tf_op jit(solution)/shard_map/convert_element_type | solution.py:59
  1.9 1.3 %collective-permute-start = (bf16[64,128]{1,0:T(8,128)(2,1)S(1)}, bf16[64,128]{1,0:T(8,128)(2,1)S(1)}, u32[]{:S(2)}, u32[]{:S(2)}) collective-permute-start(bf16[64,128]{1,0:T(8,128)(2,1)S(1)} %slice_bitcast_fusion.1), channel_id=1, source_target_pairs={{4,0},{8,4},{12,8},{16,12},{20,16},{24,20},{28,24},{5,1},{9,5},{13... | collective-permute-start | bytes 49160 | tf_op jit(solution)/shard_map/ppermute | solution.py:10
  3.2 1.0 fusion.23
  4.2 1.3 %fusion.25 = f32[16,64,128]{2,1,0:T(8,128)S(1)} fusion(bf16[16,64,128]{2,1,0:T(8,128)(2,1)S(1)} %multiply_convert_fusion, bf16[16,128,128]{2,1,0:T(8,128)(2,1)} %param.17), kind=kOutput, calls=%fused_computation.56 | convolution fusion | flops 33554432 | bytes 1310720 | tf_op jit(solution)/shard_map/btp,bpq->btq/dot_general | solution.py:68
  5.5 0.8 iota_compare_fusion.1
  6.4 0.0 collective-permute-done
  6.4 1.0 fusion.24
  7.4 0.3 convolution_negate_fusion
  7.7 3.8 %collective-permute-start.1 = (f32[64,128]{1,0:T(8,128)S(1)}, f32[64,128]{1,0:T(8,128)S(1)}, u32[]{:S(2)}, u32[]{:S(2)}) collective-permute-start(f32[64,128]{1,0:T(8,128)S(1)} %slice_bitcast_fusion), channel_id=1, source_target_pairs={{0,4},{4,8},{8,12},{12,16},{16,20},{20,24},{24,28},{1,5},{5,9},{9,... | collective-permute-start | bytes 98312 | tf_op jit(solution)/shard_map/ppermute | solution.py:10
  11.5 0.0 copy-done.2
  11.5 0.1 iota_compare_fusion
  11.8 0.6 collective-permute-done.1
  12.4 0.3 fusion.4
  12.7 0.0 copy-done
  12.7 0.0 copy-start.1
  12.7 0.5 convolution_bitcast_fusion
  13.2 26.5 %all-reduce.2 = bf16[64,512]{1,0:T(8,128)(2,1)S(1)} all-reduce(f32[64,512]{1,0:T(8,128)S(1)} %convolution_bitcast_fusion), channel_id=1, replica_groups=mesh['bus'=8,'period'=4] {'bus'}, use_global_device_ids=true, to_apply=%region_0.0 | all-reduce | flops 32768 | bytes 196608 | tf_op jit(solution)/shard_map/psum | solution.py:80
  39.7 2.8 %fusion.1 = f32[8,1,512]{2,1,0:T(1,128)S(1)} fusion(bf16[1,8,512,512]{3,2,1,0:T(8,128)(2,1)} %param.22, bf16[8,512,1]{1,0,2:T(8,128)(2,1)S(1)} %fusion.17), kind=kOutput, calls=%fused_computation.12 | convolution fusion | flops 4194304 | bytes 4218880 | tf_op jit(solution)/shard_map/tm,tmn->tn/dot_general | solution.py:83
  42.5 7.1 %while.47 = (s32[]{:T(128)}, f32[512]{0:T(512)S(1)}, f32[512]{0:T(512)S(1)}, f32[8,512]{1,0:T(8,128)S(1)}, f32[8,512]{1,0:T(8,128)S(1)}, /*index=5*/f32[8,512]{1...) while((s32[]{:T(128)}, f32[512]{0:T(512)S(1)}, f32[512]{0:T(512)S(1)}, f32[8,512]{1,0:T(8,128)S(1)}, ...), condition=%wide.region_2.3_spmd.clone, body=%wide.region_1.2_spmd.clone.sunk | while | flops 2563 | bytes 28787 | solution.py:97
  42.5 0.7 constant_dynamic-slice_fusion.9
  43.3 0.1 dynamic_update_slice.12
  43.3 0.1 dynamic_update_slice.11
  43.4 0.7 constant_dynamic-slice_fusion.9
  44.2 0.1 dynamic_update_slice.12
  44.2 0.1 dynamic_update_slice.11
  44.3 0.7 constant_dynamic-slice_fusion.9
  45.0 0.1 dynamic_update_slice.12
  45.1 0.1 dynamic_update_slice.11
  45.2 0.7 constant_dynamic-slice_fusion.9
  45.9 0.1 dynamic_update_slice.12
  46.0 0.1 dynamic_update_slice.11
  46.1 0.7 constant_dynamic-slice_fusion.9
  46.8 0.1 dynamic_update_slice.12
  46.9 0.1 dynamic_update_slice.11
  47.0 0.7 constant_dynamic-slice_fusion.9
  47.7 0.1 dynamic_update_slice.12
  47.8 0.1 dynamic_update_slice.11
  47.9 0.7 constant_dynamic-slice_fusion.9
  48.6 0.1 dynamic_update_slice.12
  48.7 0.1 dynamic_update_slice.11
  48.8 0.7 constant_dynamic-slice_fusion.9
  49.5 0.1 dynamic_update_slice.12
  49.6 0.1 dynamic_update_slice.11
  49.7 10.4 %all-gather.3 = f32[8,1,512]{2,1,0:T(1,128)S(1)} all-gather(f32[1,1,512]{2,1,0:T(1,128)S(1)} %bitcast.67), channel_id=3, replica_groups=mesh['bus'=8,'period'=4] {'bus'}, dimensions={0}, use_global_device_ids=true | all-gather | bytes 18432 | tf_op jit(solution)/shard_map/all_gather | solution.py:15
  60.0 7.7 %all-gather.2 = f32[8,1,512]{2,1,0:T(1,128)S(1)} all-gather(f32[1,1,512]{2,1,0:T(1,128)S(1)} %bitcast.69), channel_id=2, replica_groups=mesh['bus'=8,'period'=4] {'bus'}, dimensions={0}, use_global_device_ids=true | all-gather | bytes 18432 | tf_op jit(solution)/shard_map/all_gather | solution.py:15
  67.7 0.4 while.48
  68.2 13.2 %all-reduce = (f32[1,512]{1,0:T(1,128)S(1)}, f32[1,512]{1,0:T(1,128)S(1)}) all-reduce(f32[1,512]{1,0:T(1,128)S(1)} %bitcast.83, f32[1,512]{1,0:T(1,128)S(1)} %bitcast.82), channel_id=1, replica_groups=mesh['bus'=8,'period'=4] {'bus'}, use_global_device_ids=true, to_apply=%region_5.6 | all-reduce | flops 1024 | bytes 8192 | tf_op jit(solution)/shard_map/psum | solution.py:32
  81.4 12.1 %all-gather.5 = f32[4,1,512]{2,1,0:T(1,128)S(1)} all-gather(f32[1,1,512]{2,1,0:T(1,128)S(1)} %bitcast.86), channel_id=1, replica_groups=mesh['bus'=8,'period'=4] {'period'}, dimensions={0}, use_global_device_ids=true | all-gather | bytes 10240 | tf_op jit(solution)/shard_map/all_gather | solution.py:15
  93.5 11.9 %all-gather.4 = f32[4,1,512]{2,1,0:T(1,128)S(1)} all-gather(f32[1,1,512]{2,1,0:T(1,128)S(1)} %bitcast.85), channel_id=1, replica_groups=mesh['bus'=8,'period'=4] {'period'}, dimensions={0}, use_global_device_ids=true | all-gather | bytes 10240 | tf_op jit(solution)/shard_map/all_gather | solution.py:15
  105.3 0.2 while.49
  105.6 0.6 add_bitcast_fusion
  106.2 0.0 copy-done.1
  (51 shorter events, 0.5 us)
Async XLA Ops:
  0.6 12.0 %copy-start = (bf16[16,128,512]{2,1,0:T(8,128)(2,1)S(1)}, bf16[16,128,512]{2,1,0:T(8,128)(2,1)}, u32[]{:S(2)}) copy-start(bf16[16,128,512]{2,1,0:T(8,128)(2,1)} %param.21) | copy-start | bytes 6291460
  0.6 10.9 %copy-start.2 = (s32[16,16]{1,0:T(8,128)S(1)}, s32[16,16]{1,0:T(8,128)}, u32[]{:S(2)}) copy-start(s32[16,16]{1,0:T(8,128)} %param.18) | copy-start | bytes 3076
  1.9 4.5 %collective-permute-start = (bf16[64,128]{1,0:T(8,128)(2,1)S(1)}, bf16[64,128]{1,0:T(8,128)(2,1)S(1)}, u32[]{:S(2)}, u32[]{:S(2)}) collective-permute-start(bf16[64,128]{1,0:T(8,128)(2,1)S(1)} %slice_bitcast_fusion.1), channel_id=1, source_target_pairs={{4,0},{8,4},{12,8},{16,12},{20,16},{24,20},{28,24},{5,1},{9,5},{13... | collective-permute-start | bytes 49160 | tf_op jit(solution)/shard_map/ppermute | solution.py:10
  7.7 4.7 %collective-permute-start.1 = (f32[64,128]{1,0:T(8,128)S(1)}, f32[64,128]{1,0:T(8,128)S(1)}, u32[]{:S(2)}, u32[]{:S(2)}) collective-permute-start(f32[64,128]{1,0:T(8,128)S(1)} %slice_bitcast_fusion), channel_id=1, source_target_pairs={{0,4},{4,8},{8,12},{12,16},{16,20},{20,24},{24,28},{1,5},{5,9},{9,... | collective-permute-start | bytes 98312 | tf_op jit(solution)/shard_map/ppermute | solution.py:10
  12.7 93.5 %copy-start.1 = (bf16[16,64,128]{2,1,0:T(8,128)(2,1)}, bf16[16,64,128]{2,1,0:T(8,128)(2,1)S(1)}, u32[]{:S(2)}) copy-start(bf16[16,64,128]{2,1,0:T(8,128)(2,1)S(1)} %fusion.4) | copy-start | bytes 786436
where the time goes:
time: 107 us; the launch traced here: 106 us
  blocking collectives  81.7 us (76%)
  matrix products  7.18 us (7%)
  local copies, waits for them, and re-layouts  7.02 us (7%)
  starting transfers between devices  5.11 us (5%)
  other arithmetic  3.07 us (3%)
    all_gather x4, blocking collectives, entering_2(): everything = jax.tree.map(lambda part: lax.all_gather(part, axis), value)  42 us
    psum x1, blocking collectives, shards(): totals = lax.psum(partial_value, 'bus')  26.5 us
    psum x1, blocking collectives, broadcast(): return lax.psum(block, axis)  13.2 us
    dynamic_slice x8, local copies, waits for them, and re-layouts, shards(): lax.scan(advance, (zeros_row, ones_row), (retention[0], pushed))  5.84 us
    ppermute x2, starting transfers between devices, from_behind(): lax.ppermute(value, axis, [(source, source + steps) for source in range(l...  5.11 us
    dot_general x1, matrix products, shards(): jnp.einsum('tm,tmn->tn', section_in, section_gain[0], preferred_element_t...  2.83 us
  transfers between devices with their start and end apart: 2, of which 1 were waited for; matrix products, arithmetic and copies ran while one was open for 3% of the time, Pallas kernels for 0%

commit v1 on v0

--- a/solution.py
+++ b/solution.py
@@ -77,7 +77,7 @@
     partial_value = jnp.einsum(
         "btq,bqm->tm", mismatch, condense, preferred_element_type=jnp.float32
     )
-    totals = lax.psum(partial_value, "bus")
+    totals = jnp.sum(lax.all_gather(partial_value, "bus"), axis=0)
     section_sum = lax.dynamic_slice_in_dim(totals, lax.axis_index("bus") * span_rows, span_rows, 0)
     section_in = section_sum.astype(jnp.bfloat16)
     pushed = jnp.einsum(

time: 107 us -> 123 us (1.15)
  waiting for transfers between devices: 0.6 us -> 29 us
  blocking collectives: 81.7 us -> 53.8 us
  between operations: 0.9 us -> 14.3 us
  other arithmetic: 3.07 us -> 4.38 us
    all_gather x0 -> x1, waiting for transfers between devices: none -> 28.3 us  [shards(): totals = jnp.sum(lax.all_gather(partial_value, 'bus'), axis=0)]
    psum x1 -> x0, blocking collectives: 26.5 us -> none  [shards(): totals = lax.psum(partial_value, 'bus')]
    all_gather x4, blocking collectives: 42 us -> 40.6 us  [entering_2(): everything = jax.tree.map(lambda part: lax.all_gather(part, axis), value)]
    reduce_sum x0 -> x1, other arithmetic: none -> 1.32 us  [shards(): totals = jnp.sum(lax.all_gather(partial_value, 'bus'), axis=0)]
  transfers between devices with their start and end apart: 2 -> 3, of which waited for: 1 -> 2; matrix products, arithmetic and copies ran while one was open for 3% -> 3% of each run, Pallas kernels for 0% -> 0%
where the time goes in v1:
time: 123 us; the launch traced here: 122 us
  blocking collectives  53.8 us (44%)
  waiting for transfers between devices  29 us (24%)
  between operations  14.3 us (12%)
  matrix products  7.84 us (6%)
  local copies, waits for them, and re-layouts  7.02 us (6%)
  starting transfers between devices  5.15 us (4%)
  other arithmetic  4.38 us (4%)
    all_gather x4, blocking collectives, entering_2(): everything = jax.tree.map(lambda part: lax.all_gather(part, axis), value)  40.6 us
    all_gather x1, waiting for transfers between devices, shards(): totals = jnp.sum(lax.all_gather(partial_value, 'bus'), axis=0)  28.3 us
    psum x1, blocking collectives, broadcast(): return lax.psum(block, axis)  13.2 us
    dynamic_slice x8, local copies, waits for them, and re-layouts, shards(): lax.scan(advance, (zeros_row, ones_row), (retention[0], pushed))  5.84 us
    ppermute x2, starting transfers between devices, from_behind(): lax.ppermute(value, axis, [(source, source + steps) for source in range(l...  5.11 us
    dot_general x1, matrix products, shards(): jnp.einsum('tm,tmn->tn', section_in, section_gain[0], preferred_element_t...  2.83 us
  transfers between devices with their start and end apart: 3, of which 2 were waited for; matrix products, arithmetic and copies ran while one was open for 3% of the time, Pallas kernels for 0%

profile of v1, /device:TPU:0, one launch (start us, length us, event | category | flops | bytes accessed | tf_op | source)
XLA Modules:
  0.0 122.0 jit_solution(301412429448031556)
XLA Ops:
  7.2 0.0 copy-start
  7.2 0.0 copy-start.2
  7.2 0.0 all-gather.9.cloned.1.call-start
  7.2 1.2 %multiply_convert_fusion = bf16[16,64,128]{2,1,0:T(8,128)(2,1)S(1)} fusion(bf16[16,64,128]{2,1,0:T(8,128)(2,1)} %param.16, bf16[16,64,128]{2,1,0:T(8,128)(2,1)} %param.15), kind=kLoop, calls=%fused_computation.21 | loop fusion | flops 524288 | bytes 786432 | tf_op jit(solution)/shard_map/convert_element_type | solution.py:59
  8.5 1.3 %collective-permute-start = (bf16[64,128]{1,0:T(8,128)(2,1)S(1)}, bf16[64,128]{1,0:T(8,128)(2,1)S(1)}, u32[]{:S(2)}, u32[]{:S(2)}) collective-permute-start(bf16[64,128]{1,0:T(8,128)(2,1)S(1)} %slice_bitcast_fusion.1), channel_id=1, source_target_pairs={{4,0},{8,4},{12,8},{16,12},{20,16},{24,20},{28,24},{5,1},{9,5},{13... | collective-permute-start | bytes 49160 | tf_op jit(solution)/shard_map/ppermute | solution.py:10
  9.8 1.0 fusion.23
  10.8 1.3 %fusion.25 = f32[16,64,128]{2,1,0:T(8,128)S(1)} fusion(bf16[16,64,128]{2,1,0:T(8,128)(2,1)S(1)} %multiply_convert_fusion, bf16[16,128,128]{2,1,0:T(8,128)(2,1)} %param.17), kind=kOutput, calls=%fused_computation.56 | convolution fusion | flops 33554432 | bytes 1310720 | tf_op jit(solution)/shard_map/btp,bpq->btq/dot_general | solution.py:68
  12.1 0.8 iota_compare_fusion.1
  12.9 0.0 collective-permute-done
  13.0 1.0 fusion.24
  14.0 0.3 convolution_negate_fusion
  14.3 3.8 %collective-permute-start.1 = (f32[64,128]{1,0:T(8,128)S(1)}, f32[64,128]{1,0:T(8,128)S(1)}, u32[]{:S(2)}, u32[]{:S(2)}) collective-permute-start(f32[64,128]{1,0:T(8,128)S(1)} %slice_bitcast_fusion), channel_id=1, source_target_pairs={{0,4},{4,8},{8,12},{12,16},{16,20},{20,24},{24,28},{1,5},{5,9},{9,... | collective-permute-start | bytes 98312 | tf_op jit(solution)/shard_map/ppermute | solution.py:10
  18.1 0.0 copy-done.2
  18.1 0.1 iota_compare_fusion
  18.3 0.7 collective-permute-done.1
  18.9 0.3 fusion.4
  19.2 0.0 copy-done
  19.2 0.0 copy-start.1
  19.2 1.1 convolution_bitcast_fusion
  20.4 0.0 all-gather.9.cloned.1.call-update
  20.5 28.3 %all-gather.9.cloned.1.call-done = f32[512,512]{1,0:T(8,128)} async-done(((f32[64,512]{1,0:T(8,128)}), f32[512,512]{1,0:T(8,128)}) %all-gather.9.cloned.1.call-update) | async-done | bytes 1048592 | tf_op jit(solution)/shard_map/all_gather | solution.py:80
  48.8 1.3 %reduce_sum.9 = bf16[64,512]{1,0:T(8,128)(2,1)S(1)} reduce(f32[8,64,512]{2,1,0:T(8,128)} %bitcast.67, f32[]{:T(128)} %constant.70.clone.1), dimensions={0}, to_apply=%region_0.0 | reduce | flops 229376 | bytes 1114116 | tf_op jit(solution)/shard_map/reduce_sum | solution.py:80
  50.1 2.8 %fusion.1 = f32[8,1,512]{2,1,0:T(1,128)S(1)} fusion(bf16[1,8,512,512]{3,2,1,0:T(8,128)(2,1)} %param.22, bf16[8,512,1]{1,0,2:T(8,128)(2,1)S(1)} %fusion.17), kind=kOutput, calls=%fused_computation.12 | convolution fusion | flops 4194304 | bytes 4218880 | tf_op jit(solution)/shard_map/tm,tmn->tn/dot_general | solution.py:83
  52.9 0.0 copy-done.1
  52.9 7.1 %while.47 = (s32[]{:T(128)}, f32[512]{0:T(512)S(1)}, f32[512]{0:T(512)S(1)}, f32[8,512]{1,0:T(8,128)S(1)}, f32[8,512]{1,0:T(8,128)S(1)}, /*index=5*/f32[8,512]{1...) while((s32[]{:T(128)}, f32[512]{0:T(512)S(1)}, f32[512]{0:T(512)S(1)}, f32[8,512]{1,0:T(8,128)S(1)}, ...), condition=%wide.region_2.3_spmd.clone, body=%wide.region_1.2_spmd.clone.sunk | while | flops 2563 | bytes 28787 | solution.py:97
  52.9 0.7 constant_dynamic-slice_fusion.9
  53.7 0.1 dynamic_update_slice.12
  53.8 0.1 dynamic_update_slice.11
  53.9 0.7 constant_dynamic-slice_fusion.9
  54.6 0.1 dynamic_update_slice.12
  54.7 0.1 dynamic_update_slice.11
  54.7 0.7 constant_dynamic-slice_fusion.9
  55.5 0.1 dynamic_update_slice.12
  55.6 0.1 dynamic_update_slice.11
  55.6 0.7 constant_dynamic-slice_fusion.9
  56.4 0.1 dynamic_update_slice.12
  56.4 0.1 dynamic_update_slice.11
  56.5 0.7 constant_dynamic-slice_fusion.9
  57.3 0.1 dynamic_update_slice.12
  57.3 0.1 dynamic_update_slice.11
  57.4 0.7 constant_dynamic-slice_fusion.9
  58.2 0.1 dynamic_update_slice.12
  58.2 0.1 dynamic_update_slice.11
  58.3 0.7 constant_dynamic-slice_fusion.9
  59.1 0.1 dynamic_update_slice.12
  59.1 0.1 dynamic_update_slice.11
  59.2 0.7 constant_dynamic-slice_fusion.9
  60.0 0.1 dynamic_update_slice.12
  60.0 0.1 dynamic_update_slice.11
  60.1 8.9 %all-gather.4 = f32[8,1,512]{2,1,0:T(1,128)S(1)} all-gather(f32[1,1,512]{2,1,0:T(1,128)S(1)} %bitcast.69), channel_id=4, replica_groups=mesh['bus'=8,'period'=4] {'bus'}, dimensions={0}, use_global_device_ids=true | all-gather | bytes 18432 | tf_op jit(solution)/shard_map/all_gather | solution.py:15
  69.0 7.9 %all-gather.3 = f32[8,1,512]{2,1,0:T(1,128)S(1)} all-gather(f32[1,1,512]{2,1,0:T(1,128)S(1)} %bitcast.71), channel_id=3, replica_groups=mesh['bus'=8,'period'=4] {'bus'}, dimensions={0}, use_global_device_ids=true | all-gather | bytes 18432 | tf_op jit(solution)/shard_map/all_gather | solution.py:15
  76.9 0.4 while.48
  77.4 13.2 %all-reduce = (f32[1,512]{1,0:T(1,128)S(1)}, f32[1,512]{1,0:T(1,128)S(1)}) all-reduce(f32[1,512]{1,0:T(1,128)S(1)} %bitcast.85, f32[1,512]{1,0:T(1,128)S(1)} %bitcast.84), channel_id=1, replica_groups=mesh['bus'=8,'period'=4] {'bus'}, use_global_device_ids=true, to_apply=%region_5.6 | all-reduce | flops 1024 | bytes 8192 | tf_op jit(solution)/shard_map/psum | solution.py:32
  90.5 11.9 %all-gather.6 = f32[4,1,512]{2,1,0:T(1,128)S(1)} all-gather(f32[1,1,512]{2,1,0:T(1,128)S(1)} %bitcast.88), channel_id=1, replica_groups=mesh['bus'=8,'period'=4] {'period'}, dimensions={0}, use_global_device_ids=true | all-gather | bytes 10240 | tf_op jit(solution)/shard_map/all_gather | solution.py:15
  102.5 11.9 %all-gather.5 = f32[4,1,512]{2,1,0:T(1,128)S(1)} all-gather(f32[1,1,512]{2,1,0:T(1,128)S(1)} %bitcast.87), channel_id=1, replica_groups=mesh['bus'=8,'period'=4] {'period'}, dimensions={0}, use_global_device_ids=true | all-gather | bytes 10240 | tf_op jit(solution)/shard_map/all_gather | solution.py:15
  114.3 0.2 while.49
  114.5 0.6 add_bitcast_fusion
  (51 shorter events, 0.5 us)
Async XLA Ops:
  7.2 12.1 %copy-start = (bf16[16,128,512]{2,1,0:T(8,128)(2,1)S(1)}, bf16[16,128,512]{2,1,0:T(8,128)(2,1)}, u32[]{:S(2)}) copy-start(bf16[16,128,512]{2,1,0:T(8,128)(2,1)} %param.21) | copy-start | bytes 6291460
  7.2 10.9 %copy-start.2 = (s32[16,16]{1,0:T(8,128)S(1)}, s32[16,16]{1,0:T(8,128)}, u32[]{:S(2)}) copy-start(s32[16,16]{1,0:T(8,128)} %param.18) | copy-start | bytes 3076
  7.2 41.6 %all-gather.9.cloned.1.call-start = ((), (), s32[]{:S(2)}) async-start(), calls=%async_computation | async-start | bytes 1179648 | tf_op jit(solution)/shard_map/all_gather | solution.py:80
  8.5 4.5 %collective-permute-start = (bf16[64,128]{1,0:T(8,128)(2,1)S(1)}, bf16[64,128]{1,0:T(8,128)(2,1)S(1)}, u32[]{:S(2)}, u32[]{:S(2)}) collective-permute-start(bf16[64,128]{1,0:T(8,128)(2,1)S(1)} %slice_bitcast_fusion.1), channel_id=1, source_target_pairs={{4,0},{8,4},{12,8},{16,12},{20,16},{24,20},{28,24},{5,1},{9,5},{13... | collective-permute-start | bytes 49160 | tf_op jit(solution)/shard_map/ppermute | solution.py:10
  14.3 4.7 %collective-permute-start.1 = (f32[64,128]{1,0:T(8,128)S(1)}, f32[64,128]{1,0:T(8,128)S(1)}, u32[]{:S(2)}, u32[]{:S(2)}) collective-permute-start(f32[64,128]{1,0:T(8,128)S(1)} %slice_bitcast_fusion), channel_id=1, source_target_pairs={{0,4},{4,8},{8,12},{12,16},{16,20},{20,24},{24,28},{1,5},{5,9},{9,... | collective-permute-start | bytes 98312 | tf_op jit(solution)/shard_map/ppermute | solution.py:10
  19.2 33.7 %copy-start.1 = (bf16[16,64,128]{2,1,0:T(8,128)(2,1)}, bf16[16,64,128]{2,1,0:T(8,128)(2,1)S(1)}, u32[]{:S(2)}) copy-start(bf16[16,64,128]{2,1,0:T(8,128)(2,1)S(1)} %fusion.4) | copy-start | bytes 786436
Sparse Core Ops, SparseCore 0:
  20.5 28.2 all-gather.8
